TPU v7x, 256 devices: a whole 4x4x8 slice. The times are simulated.
256 devices in a mesh: seq: 32 (over y, x, core), tp: 8 (over z).
Axes of the slice: x: 4, y: 4, z: 8, core: 2. Of those that a mesh axis runs over, the one named last changes fastest.
Arguments:
- tokens: bfloat16 [8192, 4096], P('seq', 'tp'), may hold values from -11 to 11
- grad_out: bfloat16 [8192, 4096], P('seq', 'tp'), may hold values from -1.5 to 1.5
- in_weight: bfloat16 [4096, 4096], P('seq', 'tp'), may hold values from -0.09880682 to 0.09880682
- in_scale: float32 [4096], P('tp'), may hold values from 0.0008238636 to 0.010511364
- out_weight: bfloat16 [4096, 4096], P('seq', 'tp'), may hold values from -0.053943182 to 0.053943182
- out_scale: float32 [4096], replicated, may hold values from 0.00139204545 to 0.0057386364
- state_in: bfloat16 [8192, 128], P('seq'), may hold values from -0.0625 to 0.0625
- state_out: bfloat16 [8192, 128], P('seq'), may hold values from -6 to 6
- log_decay: float32 [8192, 64], P('seq', 'tp'), may hold values from -1.6 to 0
Outputs:
- grad_tokens: bfloat16 [8192, 4096], P('seq', 'tp')
- grad_in_weight: float32 [4096, 4096], P('seq', 'tp')
- grad_in_scale: float32 [4096], P('tp')
- grad_out_weight: float32 [4096, 4096], P('seq', 'tp')
- grad_out_scale: float32 [4096], P('seq')
All inputs are finite; a program needn't handle non-finite values.
Results may differ from a plain program's by a relative error of at most 0.027.
Values may be sent and summed in bfloat16 or wider, within the bound.
No kernel may reach another device: no remote copies, remote signals or barrier semaphores. Data moves between devices by JAX's collectives and lax.ppermute only.
A program may use at most 128 MiB of HBM per device.

v0:
```python
import jax
import jax.numpy as jnp
from jax import lax
from jax.sharding import PartitionSpec as P

D = 4096
HEADS = 64
HEAD_DIM = 64
STRETCH = 256
QMAX = 7
precise = lax.Precision.HIGHEST


def prefix(array, axis, join, neutral, backward):
    count = lax.axis_size(axis)
    place = lax.axis_index(axis)
    ahead = count - 1 - place if backward else place
    gathered = jax.tree.map(
        lambda a, kind: lax.all_gather(a.astype(kind), axis), array, (jnp.bfloat16, jnp.bfloat16)
    )
    state = jax.tree.map(lambda a, e: jnp.zeros_like(a) + jnp.asarray(e, a.dtype), array, neutral)

    def one(turn, state):
        source = count - 1 - turn if backward else turn
        return join(
            state,
            jax.tree.map(
                lambda a, own: lax.dynamic_index_in_dim(a, source, 0, False).astype(own.dtype),
                gathered,
                array,
            ),
        )

    return lax.fori_loop(0, ahead, one, state)


def quantize(weight, channel_scale):
    ratios = weight.astype(jnp.float32) / channel_scale
    clipped = jnp.clip(ratios, -QMAX, QMAX)
    levels = jnp.floor(clipped + 0.5)
    inside = jnp.abs(ratios) <= QMAX
    slopes = jnp.where(inside, levels - ratios, levels)
    return (levels, slopes, inside.astype(jnp.float32))


def stretch_terms(decay_logs, inputs_f, outputs_f):
    cumul = jnp.cumsum(decay_logs, axis=0)
    ending = cumul[-1]
    spread = cumul[:, None, :] - cumul[None, :, :]
    length = decay_logs.shape[0]
    causal = jnp.arange(length)[:, None] >= jnp.arange(length)[None, :]
    mixing = jnp.exp(jnp.where(causal[:, :, None], spread, -jnp.inf))
    intersection = jnp.dot(outputs_f, inputs_f.T, precision=precise)
    return (cumul, ending, mixing * intersection[:, :, None])


def forward_step(carried, pieces):
    values, cumul, ending, weights, inputs_f, outputs_f = pieces
    inner = jnp.einsum("sth,thp->shp", weights, values, precision=precise)
    outer = jnp.exp(cumul)[:, :, None] * jnp.einsum(
        "sn,hnp->shp", outputs_f, carried, precision=precise
    )
    fresh = jnp.einsum(
        "th,tn,thp->hnp", jnp.exp(ending[None, :] - cumul), inputs_f, values, precision=precise
    )
    return (jnp.exp(ending)[:, None, None] * carried + fresh, inner + outer)


def backward_step(carried, pieces):
    grads, cumul, ending, weights, inputs_f, outputs_f = pieces
    inner = jnp.einsum("sth,shp->thp", weights, grads, precision=precise)
    outer = jnp.exp(ending[None, :] - cumul)[:, :, None] * jnp.einsum(
        "tn,hnp->thp", inputs_f, carried, precision=precise
    )
    fresh = jnp.einsum("sh,sn,shp->hnp", jnp.exp(cumul), outputs_f, grads, precision=precise)
    return (jnp.exp(ending)[:, None, None] * carried + fresh, inner + outer)


def join_forward(earlier, later):
    return (earlier[0] * later[0], later[0][:, None, None] * earlier[1] + later[1])


def join_backward(earlier, later):
    return (earlier[0] * later[0], later[1] + later[0][:, None, None] * earlier[1])


def per_device(
    tokens, grad_out, in_weight, in_scale, out_weight, out_scale, state_in, state_out, log_decay
):
    local_rows = tokens.shape[0]
    heads_here = log_decay.shape[1]
    width_here = in_scale.shape[0]
    head_size = width_here // heads_here
    state_size = state_in.shape[1]
    weight_rows = in_weight.shape[0]
    blocks = local_rows // STRETCH
    row_start = lax.axis_index("seq") * weight_rows
    out_scale_rows = lax.dynamic_slice_in_dim(out_scale, row_start, weight_rows)
    in_levels, in_slopes, in_inside = quantize(in_weight, in_scale[None, :])
    out_levels, out_slopes, out_inside = quantize(out_weight, out_scale_rows[:, None])
    in_codes = lax.all_gather(in_levels.astype(jnp.bfloat16), "seq", axis=0, tiled=True)
    out_codes = lax.all_gather(out_levels.astype(jnp.bfloat16), "seq", axis=0, tiled=True)
    features = lax.all_gather(tokens, "tp", axis=1, tiled=True)
    cotangent = lax.all_gather(grad_out, "tp", axis=1, tiled=True)
    projected = jnp.dot(features, in_codes, preferred_element_type=jnp.float32) * in_scale[None, :]
    scaled_grad = (cotangent.astype(jnp.float32) * out_scale[None, :]).astype(jnp.bfloat16)
    grad_mixed = jnp.dot(scaled_grad, out_codes, preferred_element_type=jnp.float32)
    inputs_full = state_in.astype(jnp.float32)
    outputs_full = state_out.astype(jnp.float32)
    decay_blocks = log_decay.reshape(blocks, STRETCH, heads_here)
    input_blocks = inputs_full.reshape(blocks, STRETCH, state_size)
    output_blocks = outputs_full.reshape(blocks, STRETCH, state_size)
    cumul, ending, weights = jax.vmap(stretch_terms)(decay_blocks, input_blocks, output_blocks)
    value_blocks = projected.reshape(blocks, STRETCH, heads_here, head_size)
    grad_blocks = grad_mixed.reshape(blocks, STRETCH, heads_here, head_size)
    empty = jnp.zeros((heads_here, state_size, head_size), jnp.float32)
    local_state, mixed_local = lax.scan(
        forward_step, empty, (value_blocks, cumul, ending, weights, input_blocks, output_blocks)
    )
    local_grad_state, grad_local = lax.scan(
        backward_step,
        empty,
        (grad_blocks, cumul, ending, weights, input_blocks, output_blocks),
        reverse=True,
    )
    running = jnp.cumsum(log_decay, axis=0)
    device_total = running[-1]
    device_decay = jnp.exp(device_total)
    identity = (jnp.ones_like(device_decay), empty)
    entering = prefix((device_decay, local_state), "seq", join_forward, identity, False)[1]
    leaving = prefix((device_decay, local_grad_state), "seq", join_backward, identity, True)[1]
    mixed = mixed_local.reshape(local_rows, heads_here, head_size) + jnp.exp(running)[
        :, :, None
    ] * jnp.einsum("tn,hnp->thp", outputs_full, entering, precision=precise)
    grad_values = grad_local.reshape(local_rows, heads_here, head_size) + jnp.exp(
        device_total[None, :] - running
    )[:, :, None] * jnp.einsum("tn,hnp->thp", inputs_full, leaving, precision=precise)
    mixed = mixed.reshape(local_rows, width_here)
    grad_values = grad_values.reshape(local_rows, width_here)
    mixed_b = mixed.astype(jnp.bfloat16)
    grad_b = grad_values.astype(jnp.bfloat16)
    grad_scaled = (grad_values * in_scale[None, :]).astype(jnp.bfloat16)
    piece = features
    in_total = lax.psum_scatter(
        jnp.einsum("td,tc->dc", piece, grad_b, preferred_element_type=jnp.float32).astype(
            jnp.bfloat16
        ),
        "seq",
        scatter_dimension=0,
        tiled=True,
    ).astype(jnp.float32)
    piece = cotangent
    out_total = lax.psum_scatter(
        jnp.einsum("td,tc->dc", piece, mixed_b, preferred_element_type=jnp.float32).astype(
            jnp.bfloat16
        ),
        "seq",
        scatter_dimension=0,
        tiled=True,
    ).astype(jnp.float32)
    partial_tokens = jnp.einsum(
        "tc,dc->td", grad_scaled, in_codes, preferred_element_type=jnp.float32
    )
    grad_tokens = lax.psum_scatter(
        partial_tokens.astype(jnp.bfloat16), "tp", scatter_dimension=1, tiled=True
    )
    in_part = jnp.sum(in_total * in_slopes, axis=0)
    out_part = jnp.sum(out_total * out_slopes, axis=1)
    in_sum = lax.psum(in_part, "seq")
    out_sum = lax.psum(out_part, "tp")
    grad_in_scale = in_sum / jnp.sqrt(jnp.float32(D * QMAX))
    grad_out_scale = out_sum / jnp.sqrt(jnp.float32(HEADS * HEAD_DIM * QMAX))
    return (
        grad_tokens,
        in_total * in_inside,
        grad_in_scale,
        out_total * out_inside,
        grad_out_scale,
    )


def solution(mesh):
    placed = (
        P("seq", "tp"),
        P("seq", "tp"),
        P("seq", "tp"),
        P("tp"),
        P("seq", "tp"),
        P(),
        P("seq", None),
        P("seq", None),
        P("seq", "tp"),
    )
    return jax.shard_map(
        per_device,
        mesh=mesh,
        in_specs=placed,
        out_specs=(P("seq", "tp"), P("seq", "tp"), P("tp"), P("seq", "tp"), P("seq")),
        check_vma=False,
    )
```

profile of v0, /device:TPU:6, one launch (start us, length us, event | category | flops | bytes accessed | tf_op | source)
XLA Modules:
  0.0 612.6 jit_solution(15400213899961906926)
XLA Ops:
  8.0 1.0 copy.60
  10.5 1.3 reduce-window.14
  12.4 41.5 %all-gather.10.cloned.1.call-done = bf16[256,4096]{1,0:T(8,128)(2,1)} async-done(((bf16[256,512]{1,0:T(8,128)(2,1)}), bf16[256,4096]{1,0:T(8,128)(2,1)}) %all-gather.10.cloned.1.call-update) | async-done | bytes 2097168 | tf_op jit(solution)/shard_map/all_gather | solution.py:104
  53.9 55.4 %all-gather.12.cloned.1.call-done = bf16[4096,512]{0,1:T(8,128)(2,1)} async-done(((bf16[128,512]{0,1:T(8,128)(2,1)}), bf16[4096,512]{0,1:T(8,128)(2,1)}) %all-gather.12.cloned.1.call-update) | async-done | bytes 4194320 | tf_op jit(solution)/shard_map/all_gather | solution.py:102
  109.3 4.1 fusion.2
  113.4 1.0 fusion.20
  116.2 18.9 %all-gather.2 = bf16[32,1,8]{2,1,0:T(2,128)(2,1)S(1)} all-gather(bf16[1,1,8]{2,1,0:T(2,128)(2,1)S(1)} %bitcast.154), channel_id=1, replica_groups=mesh['seq'=32,'tp'=8] {'seq'}, dimensions={0}, use_global_device_ids=true | all-gather | bytes 528 | tf_op jit(solution)/shard_map/all_gather | solution.py:19
  135.6 1.8 fusion.6
  137.5 28.1 %all-gather.18.cloned.1.call-done = bf16[256,128,64]{1,2,0:T(8,128)(2,1)} async-done(((bf16[8,128,64]{1,2,0:T(8,128)(2,1)}), bf16[256,128,64]{1,2,0:T(8,128)(2,1)}) %all-gather.18.cloned.1.call-update) | async-done | bytes 4194320 | tf_op jit(solution)/shard_map/all_gather | solution.py:19
  165.6 32.6 %while.16 = (s32[]{:T(128)}, f32[8,128,64]{2,1,0:T(8,128)S(1)}, s32[]{:T(128)}, bf16[32,8,128,64]{2,3,1,0:T(8,128)(2,1)}, bf16[32,8]{1,0:T(8,128)(2,1)S(1)}, /*index=5*/s32[]{:T(128)}, s32[]{:T(128)}, s32[]{:T(128)}, s32[]{:T(128)}) while((s32[]{:T(128)}, f32[8,128,64]{2,1,0:T(8,128)S(1)}, s32[]{:T(128)}, bf16[32,8,128,64]{2,3,1,0:T(8,128)(2,1)}, ...), condition=%wide.region_5.6_spmd, body=%wide.region_4.5_spmd.sunk | while | flops 196622 | bytes 1179883 | solution.py:34
  165.6 0.9 constant_dynamic-slice_fusion.4
  166.9 0.9 constant_dynamic-slice_fusion.4
  168.2 0.9 constant_dynamic-slice_fusion.4
  169.5 0.9 constant_dynamic-slice_fusion.4
  170.8 0.9 constant_dynamic-slice_fusion.4
  172.1 0.9 constant_dynamic-slice_fusion.4
  173.4 0.9 constant_dynamic-slice_fusion.4
  174.7 0.9 constant_dynamic-slice_fusion.4
  176.0 0.9 constant_dynamic-slice_fusion.4
  177.3 0.9 constant_dynamic-slice_fusion.4
  178.6 0.9 constant_dynamic-slice_fusion.4
  179.9 0.9 constant_dynamic-slice_fusion.4
  181.3 0.9 constant_dynamic-slice_fusion.4
  182.6 0.9 constant_dynamic-slice_fusion.4
  183.9 0.9 constant_dynamic-slice_fusion.4
  185.2 0.9 constant_dynamic-slice_fusion.4
  186.5 0.9 constant_dynamic-slice_fusion.4
  187.8 0.9 constant_dynamic-slice_fusion.4
  189.1 0.9 constant_dynamic-slice_fusion.4
  190.4 0.9 constant_dynamic-slice_fusion.4
  191.7 0.9 constant_dynamic-slice_fusion.4
  193.0 0.9 constant_dynamic-slice_fusion.4
  194.3 0.9 constant_dynamic-slice_fusion.4
  195.6 0.9 constant_dynamic-slice_fusion.4
  196.9 0.9 constant_dynamic-slice_fusion.4
  199.3 8.6 %all-gather.16.cloned.1.call-done = bf16[256,4096]{1,0:T(8,128)(2,1)} async-done(((bf16[256,512]{1,0:T(8,128)(2,1)}), bf16[256,4096]{1,0:T(8,128)(2,1)}) %all-gather.16.cloned.1.call-update) | async-done | bytes 2097168 | tf_op jit(solution)/shard_map/all_gather | solution.py:103
  207.9 4.8 fusion
  212.7 6.5 %copy.81 = bf16[4096,512]{1,0:T(8,128)(2,1)} copy(bf16[4096,512]{0,1:T(8,128)(2,1)} %fusion) | data formatting | bytes 8388608
  219.2 0.8 copy-done.7
  220.2 87.2 %reduce-scatter.10.cloned.1.call-done = bf16[128,512]{1,0:T(8,128)(2,1)} async-done(((bf16[4096,512]{1,0:T(8,128)(2,1)}), bf16[128,512]{1,0:T(8,128)(2,1)}) %reduce-scatter.10.cloned.1.call-update) | async-done | bytes 131088
  307.4 1.0 copy.82
  308.4 0.9 fusion.34
  309.3 54.8 %all-gather.14.cloned.1.call-done = bf16[4096,512]{0,1:T(8,128)(2,1)} async-done(((bf16[128,512]{0,1:T(8,128)(2,1)}), bf16[4096,512]{0,1:T(8,128)(2,1)}) %all-gather.14.cloned.1.call-update) | async-done | bytes 4194320 | tf_op jit(solution)/shard_map/all_gather | solution.py:101
  364.1 3.5 convolution_multiply_fusion
  368.4 1.0 fusion.19
  369.6 3.5 fusion.7
  373.0 47.4 %all-gather.20.cloned.1.call-done = bf16[256,128,64]{1,2,0:T(8,128)(2,1)} async-done(((bf16[8,128,64]{1,2,0:T(8,128)(2,1)}), bf16[256,128,64]{1,2,0:T(8,128)(2,1)}) %all-gather.20.cloned.1.call-update) | async-done | bytes 4194320 | tf_op jit(solution)/shard_map/all_gather | solution.py:19
  420.5 8.0 %while.17 = (s32[]{:T(128)}, f32[8,128,64]{2,1,0:T(8,128)S(1)}, s32[]{:T(128)}, bf16[32,8]{1,0:T(8,128)(2,1)S(1)}, bf16[32,8,128,64]{2,3,1,0:T(8,128)(2,1)}, /*index=5*/s32[]{:T(128)}, s32[]{:T(128)}, s32[]{:T(128)}) while((s32[]{:T(128)}, f32[8,128,64]{2,1,0:T(8,128)S(1)}, s32[]{:T(128)}, bf16[32,8]{1,0:T(8,128)(2,1)S(1)}, ...), condition=%wide.region_11.12_spmd, body=%wide.region_10.11_spmd.sunk | while | flops 196621 | bytes 1179863 | solution.py:34
  420.5 0.9 constant_dynamic-slice_fusion.5
  421.8 0.9 constant_dynamic-slice_fusion.5
  423.1 0.9 constant_dynamic-slice_fusion.5
  424.4 0.9 constant_dynamic-slice_fusion.5
  425.7 0.9 constant_dynamic-slice_fusion.5
  427.1 0.9 constant_dynamic-slice_fusion.5
  430.1 3.2 fusion.1
  433.4 6.5 %copy.83 = bf16[4096,512]{1,0:T(8,128)(2,1)} copy(bf16[4096,512]{0,1:T(8,128)(2,1)} %fusion.1) | data formatting | bytes 8388608
  440.1 4.9 convolution_convert_fusion.2
  445.0 0.8 copy.72
  445.8 83.4 %psum.14 = f32[512]{0:T(512)S(1)} all-reduce(f32[512]{0:T(512)S(1)} %get-tuple-element.273), channel_id=1, replica_groups=mesh['seq'=32,'tp'=8] {'seq'}, use_global_device_ids=true, to_apply=%region_9.10 | all-reduce | flops 512 | bytes 4096 | tf_op jit(solution)/shard_map/psum | solution.py:169
  529.8 31.0 %reduce-scatter.12.cloned.1.call-done = bf16[128,512]{1,0:T(8,128)(2,1)} async-done(((bf16[4096,512]{1,0:T(8,128)(2,1)}), bf16[128,512]{1,0:T(8,128)(2,1)}) %reduce-scatter.12.cloned.1.call-update) | async-done | bytes 131088
  560.8 1.0 copy.84
  562.0 0.8 copy.73
  562.8 17.4 %psum.15 = f32[128]{0:T(128)S(1)} all-reduce(f32[128]{0:T(128)S(1)} %get-tuple-element.275), channel_id=1, replica_groups=mesh['seq'=32,'tp'=8] {'tp'}, use_global_device_ids=true, to_apply=%region_14.15 | all-reduce | flops 128 | bytes 1024 | tf_op jit(solution)/shard_map/psum | solution.py:170
  580.7 25.3 %reduce-scatter.8.cloned.1.call-done = bf16[256,512]{1,0:T(8,128)(2,1)} async-done(((bf16[256,4096]{1,0:T(8,128)(2,1)}), bf16[256,512]{1,0:T(8,128)(2,1)}) %reduce-scatter.8.cloned.1.call-update) | async-done | bytes 262160 | tf_op jit(solution)/shard_map/reduce_scatter | solution.py:164
  (163 shorter events, 21.0 us)
Async XLA Ops:
  7.2 128.3 %copy-start = (bf16[256,128]{1,0:T(8,128)(2,1)S(1)}, bf16[256,128]{1,0:T(8,128)(2,1)}, u32[]{:S(2)}) copy-start(bf16[256,128]{1,0:T(8,128)(2,1)} %param.19) | copy-start | bytes 196612
  7.2 46.7 %all-gather.10.cloned.1.call-start = ((), (), s32[]{:S(2)}) async-start(), calls=%async_computation.3 | async-start | bytes 2359296 | tf_op jit(solution)/shard_map/all_gather | solution.py:104
  7.9 101.4 %all-gather.12.cloned.1.call-start = ((), (), s32[]{:S(2)}) async-start(), calls=%async_computation.4 | async-start | bytes 4325376 | tf_op jit(solution)/shard_map/all_gather | solution.py:102
  10.5 155.0 %all-gather.18.cloned.1.call-start = ((), (), s32[]{:S(2)}) async-start(), calls=%async_computation.8 | async-start | bytes 4325376 | tf_op jit(solution)/shard_map/all_gather | solution.py:19
  12.4 101.1 %copy-start.3 = (bf16[256,128]{1,0:T(8,128)(2,1)S(1)}, bf16[256,128]{1,0:T(8,128)(2,1)}, u32[]{:S(2)}) copy-start(bf16[256,128]{1,0:T(8,128)(2,1)} %param.20) | copy-start | bytes 196612
  12.4 102.8 %copy-start.8 = (f32[256,8]{0,1:T(8,128)S(1)}, f32[256,8]{0,1:T(8,128)}, u32[]{:S(2)}) copy-start(f32[256,8]{0,1:T(8,128)} %param.21) | copy-start | bytes 24580
  114.5 93.4 %all-gather.16.cloned.1.call-start = ((), (), s32[]{:S(2)}) async-start(), calls=%async_computation.7 | async-start | bytes 2359296 | tf_op jit(solution)/shard_map/all_gather | solution.py:103
  115.1 192.3 %reduce-scatter.10.cloned.1.call-start = ((), (), s32[]{:S(2)}) async-start(), calls=%async_computation.10 | async-start | bytes 4325376
  135.6 30.0 %copy-start.5 = (f32[256,256]{1,0:T(8,128)}, f32[256,256]{1,0:T(8,128)S(1)}, u32[]{:S(2)}) copy-start(f32[256,256]{1,0:T(8,128)S(1)} %fusion.57) | copy-start | bytes 786436
  219.2 0.9 copy-start.7
  219.2 89.2 %copy-start.9 = (f32[512]{0:T(512)S(1)}, f32[512]{0:T(512)}, u32[]{:S(2)}) copy-start(f32[512]{0:T(512)} %param.16) | copy-start | bytes 6148
  219.2 145.0 %copy-start.2 = (bf16[256,4096]{1,0:T(8,128)(2,1)S(1)}, bf16[256,4096]{1,0:T(8,128)(2,1)}, u32[]{:S(2)}) copy-start(bf16[256,4096]{1,0:T(8,128)(2,1)} %all-gather.16.cloned.1.call-done) | copy-start | bytes 6291460
  219.2 145.0 %all-gather.14.cloned.1.call-start = ((), (), s32[]{:S(2)}) async-start(), calls=%async_computation.5 | async-start | bytes 4325376 | tf_op jit(solution)/shard_map/all_gather | solution.py:101
  309.3 60.3 %copy-start.6 = (f32[256,256]{1,0:T(8,128)S(1)}, f32[256,256]{1,0:T(8,128)}, u32[]{:S(2)}) copy-start(f32[256,256]{1,0:T(8,128)} %copy-done.5) | copy-start | bytes 786436
  309.3 111.2 %all-gather.20.cloned.1.call-start = ((), (), s32[]{:S(2)}) async-start(), calls=%async_computation.9 | async-start | bytes 4325376 | tf_op jit(solution)/shard_map/all_gather | solution.py:19
  367.6 0.8 copy-start.4
  369.5 191.3 %reduce-scatter.12.cloned.1.call-start = ((), (), s32[]{:S(2)}) async-start(), calls=%async_computation.11 | async-start | bytes 4325376
  428.5 1.6 copy-start.1
  439.9 166.1 %reduce-scatter.8.cloned.1.call-start = ((), (), s32[]{:S(2)}) async-start(), calls=%async_computation.6 | async-start | bytes 2359296 | tf_op jit(solution)/shard_map/reduce_scatter | solution.py:164
Sparse Core Ops, SparseCore 0:
  9.8 44.0 all-gather.9
  56.9 52.3 all-gather.11
  114.6 50.8 all-gather.17
  167.2 40.6 all-gather.15
  219.3 88.0 reduce-scatter.9
  310.6 53.5 all-gather.13
  369.6 50.7 all-gather.19
  440.0 120.7 reduce-scatter.11
  563.9 42.0 reduce-scatter.7
where the time goes:
time: 614 us; the launch traced here: 613 us
  waiting for transfers between devices  381 us (62%)
  blocking collectives  120 us (20%)
  local copies, waits for them, and re-layouts  55.6 us (9%)
  matrix products  30.2 us (5%)
  between operations  14.1 us (2%)
  other arithmetic  10.6 us (2%)
    unnamed x11, waiting for transfers between devices  119 us
    psum x1, blocking collectives, per_device(): in_sum = lax.psum(in_part, 'seq')  83.4 us
    all_gather x2, waiting for transfers between devices, prefix(): lax.all_gather(a.astype(kind), axis)  75.5 us
    all_gather x1, waiting for transfers between devices, per_device(): lax.all_gather(out_levels.astype(jnp.bfloat16), 'seq', axis=0, tiled=True)  55.4 us
    all_gather x1, waiting for transfers between devices, per_device(): lax.all_gather(in_levels.astype(jnp.bfloat16), 'seq', axis=0, tiled=True)  54.8 us
    all_gather x1, waiting for transfers between devices, per_device(): cotangent = lax.all_gather(grad_out, 'tp', axis=1, tiled=True)  41.5 us
    dynamic_slice x62, local copies, waits for them, and re-layouts, one(): lax.dynamic_index_in_dim(a, source, 0, False).astype(own.dtype)  34 us
    reduce_scatter x1, waiting for transfers between devices, per_device(): lax.psum_scatter(partial_tokens.astype(jnp.bfloat16), 'tp', scatter_dimen...  25.3 us
  transfers between devices with their start and end apart: 9, of which 9 were waited for; matrix products, arithmetic and copies ran while one was open for 9% of the time, Pallas kernels for 0%

commit v1 on v0

--- a/solution.py
+++ b/solution.py
@@ -9,6 +9,11 @@
 STRETCH = 256
 QMAX = 7
 precise = lax.Precision.HIGHEST
+
+
+def gather_by_exchange(shard, axis, dim):
+    copies = jnp.concatenate([shard] * lax.axis_size(axis), axis=dim)
+    return lax.all_to_all(copies, axis, dim, dim, tiled=True)
 
 
 def prefix(array, axis, join, neutral, backward):
@@ -98,7 +103,7 @@
     out_scale_rows = lax.dynamic_slice_in_dim(out_scale, row_start, weight_rows)
     in_levels, in_slopes, in_inside = quantize(in_weight, in_scale[None, :])
     out_levels, out_slopes, out_inside = quantize(out_weight, out_scale_rows[:, None])
-    in_codes = lax.all_gather(in_levels.astype(jnp.bfloat16), "seq", axis=0, tiled=True)
+    in_codes = gather_by_exchange(in_levels.astype(jnp.bfloat16), "seq", 0)
     out_codes = lax.all_gather(out_levels.astype(jnp.bfloat16), "seq", axis=0, tiled=True)
     features = lax.all_gather(tokens, "tp", axis=1, tiled=True)
     cotangent = lax.all_gather(grad_out, "tp", axis=1, tiled=True)

time: 614 us -> 660 us (1.075)
  the two profiles are of different devices: /device:TPU:6 before, /device:TPU:1 now
where the time goes in v1:
time: 660 us; the launch traced here: 657 us
  waiting for transfers between devices  369 us (56%)
  blocking collectives  100 us (15%)
  other arithmetic  69.7 us (11%)
  local copies, waits for them, and re-layouts  61.7 us (9%)
  matrix products  31.6 us (5%)
  between operations  14.4 us (2%)
  starting transfers between devices  9.28 us (1%)
    reduce_scatter x1, waiting for transfers between devices, per_device(): lax.psum_scatter(jnp.einsum('td,tc->dc', piece, mixed_b, preferred_elemen...  89.6 us
    all_gather x2, waiting for transfers between devices, prefix(): lax.all_gather(a.astype(kind), axis)  74 us
    reduce_scatter x1, waiting for transfers between devices, per_device(): lax.psum_scatter(jnp.einsum('td,tc->dc', piece, grad_b, preferred_element...  66.9 us
    psum x1, blocking collectives, per_device(): in_sum = lax.psum(in_part, 'seq')  64.3 us
    all_gather x1, waiting for transfers between devices, per_device(): lax.all_gather(out_levels.astype(jnp.bfloat16), 'seq', axis=0, tiled=True)  53.3 us
    all_to_all x1, waiting for transfers between devices, gather_by_exchange(): return lax.all_to_all(copies, axis, dim, dim, tiled=True)  48.3 us
    unnamed x31, other arithmetic  36.7 us
    all_gather x1, waiting for transfers between devices, per_device(): cotangent = lax.all_gather(grad_out, 'tp', axis=1, tiled=True)  35.8 us
  transfers between devices with their start and end apart: 9, of which 7 were waited for; matrix products, arithmetic and copies ran while one was open for 4% of the time, Pallas kernels for 0%

profile of v1, /device:TPU:1, one launch (start us, length us, event | category | flops | bytes accessed | tf_op | source)
XLA Modules:
  0.0 657.2 jit_solution(6906747984982027027)
XLA Ops:
  7.2 1.7 constant_dynamic-update-slice_fusion.31
  8.9 1.6 constant_dynamic-update-slice_fusion.30
  10.5 1.6 constant_dynamic-update-slice_fusion.29
  12.1 1.6 constant_dynamic-update-slice_fusion.28
  13.8 1.6 constant_dynamic-update-slice_fusion.27
  15.4 1.6 constant_dynamic-update-slice_fusion.26
  17.0 1.6 constant_dynamic-update-slice_fusion.25
  18.6 1.7 constant_dynamic-update-slice_fusion.24
  20.3 1.6 constant_dynamic-update-slice_fusion.23
  21.9 1.6 constant_dynamic-update-slice_fusion.22
  23.5 1.6 constant_dynamic-update-slice_fusion.21
  25.2 1.6 constant_dynamic-update-slice_fusion.20
  26.8 1.6 constant_dynamic-update-slice_fusion.19
  28.4 1.6 constant_dynamic-update-slice_fusion.18
  30.0 1.6 constant_dynamic-update-slice_fusion.17
  31.7 1.6 constant_dynamic-update-slice_fusion.16
  44.6 6.4 copy.80
  51.1 8.8 %all-to-all-start = ((bf16[32,128,512]{1,2,0:T(8,128)(2,1)}), bf16[32,128,512]{1,2,0:T(8,128)(2,1)}, u32[]{:S(2)}, u32[]{:S(2)}) async-start(bf16[32,128,512]{1,2,0:T(8,128)(2,1)} %copy.80), calls=%async_computation | async-start | bytes 8388608 | tf_op jit(solution)/shard_map/all_to_all | solution.py:16
  61.8 48.3 %all-to-all-done = bf16[32,128,512]{1,2,0:T(8,128)(2,1)} async-done(((bf16[32,128,512]{1,2,0:T(8,128)(2,1)}), bf16[32,128,512]{1,2,0:T(8,128)(2,1)}, u32[]{:S(2)}, u32[]{:S(2)}) %all-to-all-start) | async-done | bytes 4194336 | tf_op jit(solution)/shard_map/all_to_all | solution.py:16
  110.1 6.5 copy.81
  116.6 4.2 convolution_multiply_fusion
  120.8 1.1 fusion.19
  123.7 22.0 %all-gather.2 = bf16[32,1,8]{2,1,0:T(2,128)(2,1)S(1)} all-gather(bf16[1,1,8]{2,1,0:T(2,128)(2,1)S(1)} %bitcast.159), channel_id=1, replica_groups=mesh['seq'=32,'tp'=8] {'seq'}, dimensions={0}, use_global_device_ids=true | all-gather | bytes 528 | tf_op jit(solution)/shard_map/all_gather | solution.py:24
  146.0 2.4 fusion.7
  148.4 26.4 %all-gather.17.cloned.1.call-done = bf16[256,128,64]{1,2,0:T(8,128)(2,1)} async-done(((bf16[8,128,64]{1,2,0:T(8,128)(2,1)}), bf16[256,128,64]{1,2,0:T(8,128)(2,1)}) %all-gather.17.cloned.1.call-update) | async-done | bytes 4194320 | tf_op jit(solution)/shard_map/all_gather | solution.py:24
  174.9 1.3 while.17
  177.3 35.8 %all-gather.9.cloned.1.call-done = bf16[256,4096]{1,0:T(8,128)(2,1)} async-done(((bf16[256,512]{1,0:T(8,128)(2,1)}), bf16[256,4096]{1,0:T(8,128)(2,1)}) %all-gather.9.cloned.1.call-update) | async-done | bytes 2097168 | tf_op jit(solution)/shard_map/all_gather | solution.py:109
  213.1 4.8 fusion.1
  217.9 6.5 copy.97
  225.2 89.6 %reduce-scatter.12.cloned.1.call-done = bf16[128,512]{1,0:T(8,128)(2,1)} async-done(((bf16[4096,512]{1,0:T(8,128)(2,1)}), bf16[128,512]{1,0:T(8,128)(2,1)}) %reduce-scatter.12.cloned.1.call-update) | async-done | bytes 131088 | tf_op jit(solution)/shard_map/reduce_scatter | solution.py:158
  314.8 2.3 fusion.34
  317.4 53.3 %all-gather.11.cloned.1.call-done = bf16[4096,512]{1,0:T(8,128)(2,1)} async-done(((bf16[128,512]{1,0:T(8,128)(2,1)}), bf16[4096,512]{1,0:T(8,128)(2,1)}) %all-gather.11.cloned.1.call-update) | async-done | bytes 4194320 | tf_op jit(solution)/shard_map/all_gather | solution.py:107
  370.6 4.0 fusion.2
  374.6 1.0 fusion.20
  376.1 2.7 fusion.6
  378.8 47.6 %all-gather.15.cloned.1.call-done = bf16[256,128,64]{1,2,0:T(8,128)(2,1)} async-done(((bf16[8,128,64]{1,2,0:T(8,128)(2,1)}), bf16[256,128,64]{1,2,0:T(8,128)(2,1)}) %all-gather.15.cloned.1.call-update) | async-done | bytes 4194320 | tf_op jit(solution)/shard_map/all_gather | solution.py:24
  426.5 59.4 %while.16 = (s32[]{:T(128)}, f32[8,128,64]{2,1,0:T(8,128)S(1)}, s32[]{:T(128)}, bf16[32,8,128,64]{2,3,1,0:T(8,128)(2,1)}, bf16[32,8]{1,0:T(8,128)(2,1)}, /*index=5*/s32[]{:T(128)}, s32[]{:T(128)}, s32[]{:T(128)}, s32[]{:T(128)}) while((s32[]{:T(128)}, f32[8,128,64]{2,1,0:T(8,128)S(1)}, s32[]{:T(128)}, bf16[32,8,128,64]{2,3,1,0:T(8,128)(2,1)}, ...), condition=%wide.region_5.6_spmd, body=%wide.region_4.5_spmd.sunk | while | flops 196622 | bytes 1179875 | solution.py:39
  426.5 1.1 constant_dynamic-slice_fusion.4
  428.6 0.9 constant_dynamic-slice_fusion.4
  432.5 0.9 constant_dynamic-slice_fusion.4
  434.5 0.9 constant_dynamic-slice_fusion.4
  438.4 0.9 constant_dynamic-slice_fusion.4
  440.4 0.9 constant_dynamic-slice_fusion.4
  442.4 0.9 constant_dynamic-slice_fusion.4
  444.4 0.9 constant_dynamic-slice_fusion.4
  446.3 0.9 constant_dynamic-slice_fusion.4
  450.3 0.9 constant_dynamic-slice_fusion.4
  452.3 0.9 constant_dynamic-slice_fusion.4
  454.3 0.9 constant_dynamic-slice_fusion.4
  458.2 0.9 constant_dynamic-slice_fusion.4
  460.2 0.9 constant_dynamic-slice_fusion.4
  464.1 0.9 constant_dynamic-slice_fusion.4
  468.1 0.9 constant_dynamic-slice_fusion.4
  470.0 0.9 constant_dynamic-slice_fusion.4
  472.0 0.9 constant_dynamic-slice_fusion.4
  474.0 0.9 constant_dynamic-slice_fusion.4
  486.5 1.4 fusion.56
  487.9 3.2 fusion
  491.2 6.5 copy.95
  497.7 4.9 convolution_convert_fusion.2
  502.6 13.7 %psum.15 = f32[128]{0:T(128)S(1)} all-reduce(f32[128]{0:T(128)S(1)} %copy-done.17), channel_id=1, replica_groups=mesh['seq'=32,'tp'=8] {'tp'}, use_global_device_ids=true, to_apply=%region_14.15 | all-reduce | flops 128 | bytes 1024 | tf_op jit(solution)/shard_map/psum | solution.py:175
  516.9 66.9 %reduce-scatter.10.cloned.1.call-done = bf16[128,512]{1,0:T(8,128)(2,1)} async-done(((bf16[4096,512]{1,0:T(8,128)(2,1)}), bf16[128,512]{1,0:T(8,128)(2,1)}) %reduce-scatter.10.cloned.1.call-update) | async-done | bytes 131088 | tf_op jit(solution)/shard_map/reduce_scatter | solution.py:149
  583.7 1.7 fusion.33
  585.5 64.3 %psum.14 = f32[512]{0:T(512)S(1)} all-reduce(f32[512]{0:T(512)S(1)} %get-tuple-element.285), channel_id=1, replica_groups=mesh['seq'=32,'tp'=8] {'seq'}, use_global_device_ids=true, to_apply=%region_9.10 | all-reduce | flops 512 | bytes 4096 | tf_op jit(solution)/shard_map/psum | solution.py:174
  (206 shorter events, 61.6 us)
Async XLA Ops:
  7.2 113.6 %copy-start = (bf16[256,128]{1,0:T(8,128)(2,1)S(1)}, bf16[256,128]{1,0:T(8,128)(2,1)}, u32[]{:S(2)}) copy-start(bf16[256,128]{1,0:T(8,128)(2,1)} %param.19) | copy-start | bytes 196612
  7.2 26.1 %copy-start.1 = (bf16[128,512]{1,0:T(8,128)(2,1)S(1)}, bf16[128,512]{1,0:T(8,128)(2,1)}, u32[]{:S(2)}) copy-start(bf16[128,512]{1,0:T(8,128)(2,1)} %param.15) | copy-start | bytes 393220
  7.2 26.1 %copy-start.2 = (f32[512]{0:T(512)S(1)}, f32[512]{0:T(512)}, u32[]{:S(2)}) copy-start(f32[512]{0:T(512)} %param.16) | copy-start | bytes 6148
  51.1 9.6 %copy-start.15 = (f32[256,8]{0,1:T(8,128)S(1)}, f32[256,8]{0,1:T(8,128)}, u32[]{:S(2)}) copy-start(f32[256,8]{0,1:T(8,128)} %param.21) | copy-start | bytes 24580
  51.1 59.0 %all-to-all-start = ((bf16[32,128,512]{1,2,0:T(8,128)(2,1)}), bf16[32,128,512]{1,2,0:T(8,128)(2,1)}, u32[]{:S(2)}, u32[]{:S(2)}) async-start(bf16[32,128,512]{1,2,0:T(8,128)(2,1)} %copy.80), calls=%async_computation | async-start | bytes 8388608 | tf_op jit(solution)/shard_map/all_to_all | solution.py:16
  59.8 56.7 %all-gather.13.cloned.1.call-start = ((), (), s32[]{:S(2)}) async-start(), calls=%async_computation.7 | async-start | bytes 2359296 | tf_op jit(solution)/shard_map/all_gather | solution.py:108
  60.6 114.3 %all-gather.17.cloned.1.call-start = ((), (), s32[]{:S(2)}) async-start(), calls=%async_computation.9 | async-start | bytes 4325376 | tf_op jit(solution)/shard_map/all_gather | solution.py:24
  61.8 84.2 %copy-start.13 = (f32[256,8]{0,1:T(8,128)}, f32[256,8]{0,1:T(8,128)S(1)}, u32[]{:S(2)}) copy-start(f32[256,8]{0,1:T(8,128)S(1)} %get-tuple-element.282) | copy-start | bytes 24580
  116.6 29.2 %copy-start.5 = (bf16[256,128]{1,0:T(8,128)(2,1)S(1)}, bf16[256,128]{1,0:T(8,128)(2,1)}, u32[]{:S(2)}) copy-start(bf16[256,128]{1,0:T(8,128)(2,1)} %param.20) | copy-start | bytes 196612
  121.9 91.2 %all-gather.9.cloned.1.call-start = ((), (), s32[]{:S(2)}) async-start(), calls=%async_computation.4 | async-start | bytes 2359296 | tf_op jit(solution)/shard_map/all_gather | solution.py:109
  122.6 192.2 %reduce-scatter.12.cloned.1.call-start = ((), (), s32[]{:S(2)}) async-start(), calls=%async_computation.11 | async-start | bytes 4325376 | tf_op jit(solution)/shard_map/reduce_scatter | solution.py:158
  123.5 22.2 %copy-start.9 = (f32[256,8]{0,1:T(8,128)}, f32[256,8]{0,1:T(8,128)S(1)}, u32[]{:S(2)}) copy-start(f32[256,8]{0,1:T(8,128)S(1)} %get-tuple-element.280) | copy-start | bytes 24580
  145.7 31.1 %copy-start.7 = (f32[256,8]{0,1:T(8,128)}, f32[256,8]{0,1:T(8,128)S(1)}, u32[]{:S(2)}) copy-start(f32[256,8]{0,1:T(8,128)S(1)} %exp.52) | copy-start | bytes 24580
  145.8 29.1 %copy-start.11 = (pred[256,256]{1,0:T(8,128)(4,1)}, pred[256,256]{1,0:T(8,128)(4,1)S(1)}, u32[]{:S(2)}) copy-start(pred[256,256]{1,0:T(8,128)(4,1)S(1)} %iota_compare_fusion) | copy-start | bytes 196612
  176.2 41.7 %copy-start.16 = (bf16[32,8]{1,0:T(8,128)(2,1)}, bf16[32,8]{1,0:T(8,128)(2,1)S(1)}, u32[]{:S(2)}) copy-start(bf16[32,8]{1,0:T(8,128)(2,1)S(1)} %get-tuple-element.437) | copy-start | bytes 1540
  224.4 0.7 copy-start.18
  224.4 90.4 %copy-start.6 = (bf16[128,512]{1,0:T(8,128)(2,1)S(1)}, bf16[128,512]{1,0:T(8,128)(2,1)}, u32[]{:S(2)}) copy-start(bf16[128,512]{1,0:T(8,128)(2,1)} %param.17) | copy-start | bytes 393220
  224.4 146.2 %copy-start.4 = (bf16[256,4096]{1,0:T(8,128)(2,1)S(1)}, bf16[256,4096]{1,0:T(8,128)(2,1)}, u32[]{:S(2)}) copy-start(bf16[256,4096]{1,0:T(8,128)(2,1)} %all-gather.9.cloned.1.call-done) | copy-start | bytes 6291460
  224.4 146.2 %all-gather.11.cloned.1.call-start = ((), (), s32[]{:S(2)}) async-start(), calls=%async_computation.5 | async-start | bytes 4325376 | tf_op jit(solution)/shard_map/all_gather | solution.py:107
  225.2 149.4 %copy-start.8 = (f32[256,8]{0,1:T(8,128)S(1)}, f32[256,8]{0,1:T(8,128)}, u32[]{:S(2)}) copy-start(f32[256,8]{0,1:T(8,128)} %copy-done.7) | copy-start | bytes 24580
  317.1 58.7 %copy-start.10 = (f32[256,8]{0,1:T(8,128)S(1)}, f32[256,8]{0,1:T(8,128)}, u32[]{:S(2)}) copy-start(f32[256,8]{0,1:T(8,128)} %copy-done.9) | copy-start | bytes 24580
  317.1 59.0 %copy-start.12 = (pred[256,256]{1,0:T(8,128)(4,1)S(1)}, pred[256,256]{1,0:T(8,128)(4,1)}, u32[]{:S(2)}) copy-start(pred[256,256]{1,0:T(8,128)(4,1)} %copy-done.11) | copy-start | bytes 196612
  317.1 59.0 %copy-start.14 = (f32[256,8]{0,1:T(8,128)S(1)}, f32[256,8]{0,1:T(8,128)}, u32[]{:S(2)}) copy-start(f32[256,8]{0,1:T(8,128)} %copy-done.13) | copy-start | bytes 24580
  317.1 109.3 %all-gather.15.cloned.1.call-start = ((), (), s32[]{:S(2)}) async-start(), calls=%async_computation.8 | async-start | bytes 4325376 | tf_op jit(solution)/shard_map/all_gather | solution.py:24
  375.7 208.0 %reduce-scatter.10.cloned.1.call-start = ((), (), s32[]{:S(2)}) async-start(), calls=%async_computation.10 | async-start | bytes 4325376 | tf_op jit(solution)/shard_map/reduce_scatter | solution.py:149
  426.4 61.5 %copy-start.3 = (bf16[256,4096]{1,0:T(8,128)(2,1)S(1)}, bf16[256,4096]{1,0:T(8,128)(2,1)}, u32[]{:S(2)}) copy-start(bf16[256,4096]{1,0:T(8,128)(2,1)} %all-gather.13.cloned.1.call-done) | copy-start | bytes 6291460
  497.7 152.7 %reduce-scatter.8.cloned.1.call-start = ((), (), s32[]{:S(2)}) async-start(), calls=%async_computation.6 | async-start | bytes 2359296 | tf_op jit(solution)/shard_map/reduce_scatter | solution.py:169
  497.7 4.9 copy-start.17
Sparse Core Ops, SparseCore 0:
  62.5 39.9 all-gather.12
  122.0 52.7 all-gather.16
  176.6 36.4 all-gather.8
  224.6 90.1 reduce-scatter.11
  318.1 52.5 all-gather.10
  375.8 50.5 all-gather.14
  497.8 85.8 reduce-scatter.9
  586.9 38.9 reduce-scatter.7
